TPU v7x, 32 devices: a whole 2x2x4 slice. The times are simulated.
32 devices in a mesh: segment: 4 (over y, x), vocab: 8 (over z, core).
Axes of the slice: x: 2, y: 2, z: 4, core: 2. Of those that a mesh axis runs over, the one named last changes fastest.
Arguments:
- trunk_out: bfloat16 [160, 7168], P(None, 'vocab'), may hold values from -12 to 12
- embeds: bfloat16 [164, 7168], P(None, 'vocab'), may hold values from -12 to 12
- token_ids: int32 [164], replicated, may hold values from 0 to 8191
- module_weight: bfloat16 [4, 2, 7168, 7168], P('segment', None, 'vocab'), may hold values from -0.046875 to 0.046875
- hidden_gain: bfloat16 [3, 7168], P(None, 'vocab'), may hold values from 0.25 to 1.75
- embed_gain: bfloat16 [3, 7168], P(None, 'vocab'), may hold values from 0.25 to 1.75
- out_gain: bfloat16 [4, 7168], P('segment'), may hold values from 0.25 to 1.75
- head_weight: bfloat16 [7168, 8192], P('segment', 'vocab'), may hold values from -0.21260502 to 0.21260502
Outputs:
- losses: float32 [4, 160], P('segment')
All inputs are finite; a program needn't handle non-finite values.
Results may differ from a plain program's by a relative error of at most 0.00095.
Values may be sent and summed in bfloat16 or wider, within the bound.
No kernel may reach another device: no remote copies, remote signals or barrier semaphores. Data moves between devices by JAX's collectives and lax.ppermute only.
A program may use at most 128 MiB of HBM per device.

v0:
```python
import jax
import jax.numpy as jnp
from jax import lax
from jax.sharding import PartitionSpec as P

D = 7168
TOK = 160
MICRO = 4
EPSILON = 1e-06


def passed_along(block, axis, distance):
    devices = range(lax.axis_size(axis))
    route = [(i - distance, i) for i in devices if i - distance in devices]
    return lax.ppermute(block, axis, route)


def combined_all(shard, axis, combine):
    everything = jax.tree.map(lambda part: lax.all_gather(part, axis), shard)
    first = jax.tree.map(lambda part: part[0], everything)

    def step(k, so_far):
        return combine(so_far, jax.tree.map(lambda part: part[k], everything))

    return lax.fori_loop(1, lax.axis_size(axis), step, first)


def merge_softmax(earlier, second):
    highest = jnp.maximum(earlier[0], second[0])
    summed = earlier[1] * jnp.exp(earlier[0] - highest) + second[1] * jnp.exp(second[0] - highest)
    return (highest, summed, earlier[2] + second[2])


def per_device(
    trunk_out, embeds, token_ids, module_weight, hidden_gain, embed_gain, out_gain, head_weight
):
    sections = lax.axis_size("segment")
    section = lax.axis_index("segment")
    shard_index = lax.axis_index("vocab")
    local_width = trunk_out.shape[1]
    micro_rows = TOK // MICRO
    vocab_width = head_weight.shape[1]
    depth_count = hidden_gain.shape[0]
    embed_float = embeds.astype(jnp.float32)
    embed_squares = lax.psum(jnp.sum(embed_float * embed_float, axis=1), "vocab")
    embed_scale = lax.rsqrt(embed_squares / D + EPSILON)
    module_index = jnp.maximum(section - 1, 0)
    module_block = module_weight[0]
    embed_scaling = lax.dynamic_index_in_dim(embed_gain, module_index, 0, keepdims=False).astype(
        jnp.float32
    )
    next_scaling = lax.dynamic_index_in_dim(
        hidden_gain, jnp.minimum(section, depth_count - 1), 0, keepdims=False
    ).astype(jnp.float32)
    out_scaling = out_gain[0].astype(jnp.float32)
    targets = lax.dynamic_slice_in_dim(token_ids, section + 1, TOK, 0) - shard_index * vocab_width
    whole_head = lax.all_gather(head_weight, "segment", axis=0, tiled=True)
    column_ids = lax.broadcasted_iota(jnp.int32, (micro_rows, vocab_width), 1)
    incoming = jnp.zeros((micro_rows, local_width), jnp.bfloat16)
    stored_tops = jnp.zeros((TOK,), jnp.float32)
    stored_totals = jnp.ones((TOK,), jnp.float32)
    stored_picks = jnp.zeros((TOK,), jnp.float32)
    for moment in range(MICRO + sections - 1):
        micro_index = moment - section
        active = (micro_index >= 0) & (micro_index < MICRO)
        first_row = jnp.clip(micro_index, 0, MICRO - 1) * micro_rows
        own_rows = lax.dynamic_slice_in_dim(trunk_out, first_row, micro_rows, 0)
        embed_rows = lax.dynamic_slice_in_dim(embed_float, first_row + section, micro_rows, 0)
        embed_factor = lax.dynamic_slice_in_dim(embed_scale, first_row + section, micro_rows, 0)
        embed_normed = (embed_rows * embed_factor[:, None] * embed_scaling).astype(jnp.bfloat16)
        partial_value = jnp.dot(incoming, module_block[0], preferred_element_type=jnp.float32)
        partial_value = partial_value + jnp.dot(
            embed_normed, module_block[1], preferred_element_type=jnp.float32
        )
        leading = section == 0
        placed = lax.dynamic_update_slice_in_dim(
            jnp.zeros((micro_rows, D), jnp.float32),
            own_rows.astype(jnp.float32),
            shard_index * local_width,
            1,
        )
        full_rows = lax.psum(jnp.where(leading, placed, partial_value), "vocab").astype(
            jnp.bfloat16
        )
        rows_float = full_rows.astype(jnp.float32)
        inverse_rms = lax.rsqrt(jnp.mean(rows_float * rows_float, axis=1, keepdims=True) + EPSILON)
        head_input = (rows_float * inverse_rms * out_scaling).astype(jnp.bfloat16)
        own_columns = lax.dynamic_slice_in_dim(
            rows_float, shard_index * local_width, local_width, 1
        )
        passed = (own_columns * inverse_rms * next_scaling).astype(jnp.bfloat16)
        incoming = passed_along(passed, "segment", 1)
        logits = jnp.dot(head_input, whole_head, preferred_element_type=jnp.float32)
        row_targets = lax.dynamic_slice_in_dim(targets, first_row, micro_rows, 0)
        row_target = jnp.sum(jnp.where(column_ids == row_targets[:, None], logits, 0.0), axis=1)
        row_top = jnp.max(logits, axis=1)
        row_total = jnp.sum(jnp.exp(logits - row_top[:, None]), axis=1)
        stored_tops = jnp.where(
            active, lax.dynamic_update_slice_in_dim(stored_tops, row_top, first_row, 0), stored_tops
        )
        stored_totals = jnp.where(
            active,
            lax.dynamic_update_slice_in_dim(stored_totals, row_total, first_row, 0),
            stored_totals,
        )
        stored_picks = jnp.where(
            active,
            lax.dynamic_update_slice_in_dim(stored_picks, row_target, first_row, 0),
            stored_picks,
        )
    merged_tops, merged_totals, merged_picks = combined_all(
        (stored_tops, stored_totals, stored_picks), "vocab", merge_softmax
    )
    losses = merged_tops + jnp.log(merged_totals) - merged_picks
    return losses[None, :]


def solution(mesh):
    in_specs = (
        P(None, "vocab"),
        P(None, "vocab"),
        P(),
        P("segment", None, "vocab", None),
        P(None, "vocab"),
        P(None, "vocab"),
        P("segment", None),
        P("segment", "vocab"),
    )
    out_specs = P("segment", None)
    return jax.shard_map(
        per_device, mesh=mesh, in_specs=in_specs, out_specs=out_specs, check_vma=False
    )
```

profile of v0, /device:TPU:5, one launch (start us, length us, event | category | flops | bytes accessed | tf_op | source)
XLA Modules:
  0.0 643.8 jit_solution(13789716217223740814)
XLA Ops:
  7.7 13.8 %psum.56 = f32[164]{0:T(256)S(1)} all-reduce(f32[164]{0:T(256)S(1)} %multiply_reduce_fusion.6), channel_id=1, replica_groups=mesh['segment'=4,'vocab'=8] {'vocab'}, use_global_device_ids=true, to_apply=%region_1.0 | all-reduce | flops 164 | bytes 1312 | tf_op jit(solution)/shard_map/psum | solution.py:45
  21.6 7.5 %fusion.12 = f32[40,7168]{1,0:T(8,128)S(1)} fusion(bf16[1,2,896,7168]{3,2,1,0:T(8,128)(2,1)} %param.13, f32[164,896]{1,0:T(8,128)S(1)} %convert_element_type.133, s32[]{:T(128)S(6)} %select_n.352, f32[896]{0:T(1024)S(1)} %fusion.139, f32[40]{0:T(128)S(1)} %get-tuple-element.231), kind=kOutput, calls=%fused_computation.16 | convolution fusion | flops 513909760 | bytes 14139908 | tf_op jit(solution)/shard_map/dot_general | solution.py:72
  30.1 5.9 fusion.67
  36.1 56.9 %all-reduce.7 = bf16[40,7168]{1,0:T(8,128)(2,1)S(1)} all-reduce(f32[40,7168]{1,0:T(8,128)S(1)} %fusion.67), channel_id=1, replica_groups=mesh['segment'=4,'vocab'=8] {'vocab'}, use_global_device_ids=true, to_apply=%region_2.3 | all-reduce | flops 286720 | bytes 1720320 | tf_op jit(solution)/shard_map/psum | solution.py:82
  99.6 8.2 %fusion.10 = f32[40,7168]{1,0:T(8,128)} fusion(bf16[1,2,896,7168]{3,2,1,0:T(8,128)(2,1)} %param.13, f32[164,896]{1,0:T(8,128)S(1)} %convert_element_type.133, s32[]{:T(128)S(6)} %select_n.360, f32[40]{0:T(128)S(1)} %get-tuple-element.230, f32[896]{0:T(1024)S(1)} %fusion.139), kind=kOutput, calls=%fused_computation.14 | convolution fusion | flops 513909760 | bytes 14139908 | tf_op jit(solution)/shard_map/dot_general | solution.py:72
  107.8 8.3 %fusion.8 = f32[40,7168]{1,0:T(8,128)} fusion(bf16[1,2,896,7168]{3,2,1,0:T(8,128)(2,1)} %param.13, f32[164,896]{1,0:T(8,128)S(1)} %convert_element_type.133, s32[]{:T(128)S(6)} %select_n.367, f32[40]{0:T(128)S(1)} %get-tuple-element.229, f32[896]{0:T(1024)S(1)} %fusion.139), kind=kOutput, calls=%fused_computation.12 | convolution fusion | flops 513909760 | bytes 14139908 | tf_op jit(solution)/shard_map/dot_general | solution.py:72
  116.0 8.3 %fusion.6 = f32[40,7168]{1,0:T(8,128)} fusion(bf16[1,2,896,7168]{3,2,1,0:T(8,128)(2,1)} %param.13, f32[164,896]{1,0:T(8,128)} %copy-done.15, s32[]{:T(128)S(6)} %select_n.374, f32[40]{0:T(128)S(1)} %get-tuple-element.228, f32[896]{0:T(1024)S(1)} %fusion.139), kind=kOutput, calls=%fused_computation.10 | convolution fusion | flops 513909760 | bytes 14139044 | tf_op jit(solution)/shard_map/dot_general | solution.py:72
  124.4 8.1 %fusion.4 = f32[40,7168]{1,0:T(8,128)} fusion(bf16[1,2,896,7168]{3,2,1,0:T(8,128)(2,1)} %param.13, f32[164,896]{1,0:T(8,128)S(1)} %copy-done.16, s32[]{:T(128)S(6)} %select_n.381, f32[40]{0:T(128)S(1)} %get-tuple-element.227, f32[896]{0:T(1024)S(1)} %fusion.139), kind=kOutput, calls=%fused_computation.8 | convolution fusion | flops 513909760 | bytes 14139908 | tf_op jit(solution)/shard_map/dot_general | solution.py:72
  141.1 4.4 fusion.64
  145.5 57.9 %all-reduce.8 = bf16[40,7168]{1,0:T(8,128)(2,1)S(1)} all-reduce(f32[40,7168]{1,0:T(8,128)} %fusion.64), channel_id=1, replica_groups=mesh['segment'=4,'vocab'=8] {'vocab'}, use_global_device_ids=true, to_apply=%region_5.6 | all-reduce | flops 286720 | bytes 1720320 | tf_op jit(solution)/shard_map/psum | solution.py:82
  210.0 8.0 %fusion.61 = f32[40,7168]{1,0:T(8,128)} fusion(f32[40,7168]{1,0:T(8,128)S(1)} %copy-done.6, f32[40,7168]{1,0:T(8,128)S(1)} %copy-done.14, bf16[40,896]{1,0:T(8,128)(2,1)S(1)} %collective-permute-done.1, bf16[1,2,896,7168]{3,2,1,0:T(8,128)(2,1)} %param.13, pred[]{:T(512)S(6)} %eq.30), kind=kOutput, calls=%fused_computation.43 | convolution fusion | flops 514375680 | bytes 16357377 | tf_op jit(solution)/shard_map/dot_general | solution.py:71
  218.1 59.6 %all-reduce.9 = bf16[40,7168]{1,0:T(8,128)(2,1)S(1)} all-reduce(f32[40,7168]{1,0:T(8,128)} %fusion.61), channel_id=1, replica_groups=mesh['segment'=4,'vocab'=8] {'vocab'}, use_global_device_ids=true, to_apply=%region_8.9 | all-reduce | flops 286720 | bytes 1720320 | tf_op jit(solution)/shard_map/psum | solution.py:82
  284.1 8.0 %fusion.58 = f32[40,7168]{1,0:T(8,128)} fusion(f32[40,7168]{1,0:T(8,128)} %convert_dynamic-update-slice_fusion.3, f32[40,7168]{1,0:T(8,128)S(1)} %copy-done.13, bf16[40,896]{1,0:T(8,128)(2,1)S(1)} %collective-permute-done.2, bf16[1,2,896,7168]{3,2,1,0:T(8,128)(2,1)} %param.13, pred[]{:T(512)S(6)} %eq.30), kind=kOutput, calls=%fused_computation.42 | convolution fusion | flops 514375680 | bytes 16357377 | tf_op jit(solution)/shard_map/dot_general | solution.py:71
  292.1 58.2 %all-reduce.10 = bf16[40,7168]{1,0:T(8,128)(2,1)S(1)} all-reduce(f32[40,7168]{1,0:T(8,128)} %fusion.58), channel_id=1, replica_groups=mesh['segment'=4,'vocab'=8] {'vocab'}, use_global_device_ids=true, to_apply=%region_11.12 | all-reduce | flops 286720 | bytes 1720320 | tf_op jit(solution)/shard_map/psum | solution.py:82
  356.9 8.0 %fusion.55 = f32[40,7168]{1,0:T(8,128)} fusion(f32[40,7168]{1,0:T(8,128)S(1)} %copy-done.8, f32[40,7168]{1,0:T(8,128)S(1)} %copy-done.12, bf16[40,896]{1,0:T(8,128)(2,1)S(1)} %collective-permute-done.3, bf16[1,2,896,7168]{3,2,1,0:T(8,128)(2,1)} %param.13, pred[]{:T(512)S(6)} %eq.30), kind=kOutput, calls=%fused_computation.41 | convolution fusion | flops 514375680 | bytes 16357377 | tf_op jit(solution)/shard_map/dot_general | solution.py:71
  365.0 59.4 %all-reduce.11 = bf16[40,7168]{1,0:T(8,128)(2,1)S(1)} all-reduce(f32[40,7168]{1,0:T(8,128)} %fusion.55), channel_id=1, replica_groups=mesh['segment'=4,'vocab'=8] {'vocab'}, use_global_device_ids=true, to_apply=%region_14.15 | all-reduce | flops 286720 | bytes 1720320 | tf_op jit(solution)/shard_map/psum | solution.py:82
  430.8 8.0 %fusion.52 = f32[40,7168]{1,0:T(8,128)} fusion(f32[40,7168]{1,0:T(8,128)} %convert_dynamic-update-slice_fusion.1, f32[40,7168]{1,0:T(8,128)S(1)} %copy-done.11, bf16[40,896]{1,0:T(8,128)(2,1)S(1)} %collective-permute-done.4, bf16[1,2,896,7168]{3,2,1,0:T(8,128)(2,1)} %param.13, pred[]{:T(512)S(6)} %eq.30), kind=kOutput, calls=%fused_computation.40 | convolution fusion | flops 514375680 | bytes 16357377 | tf_op jit(solution)/shard_map/dot_general | solution.py:71
  438.8 58.8 %all-reduce.12 = bf16[40,7168]{1,0:T(8,128)(2,1)} all-reduce(f32[40,7168]{1,0:T(8,128)} %fusion.52), channel_id=1, replica_groups=mesh['segment'=4,'vocab'=8] {'vocab'}, use_global_device_ids=true, to_apply=%region_17.18 | all-reduce | flops 286720 | bytes 1720320 | tf_op jit(solution)/shard_map/psum | solution.py:82
  505.2 8.3 %fusion.49 = f32[40,7168]{1,0:T(8,128)} fusion(f32[40,7168]{1,0:T(8,128)S(1)} %copy-done.10, f32[40,7168]{1,0:T(8,128)} %fusion, bf16[40,896]{1,0:T(8,128)(2,1)S(1)} %collective-permute-done.5, bf16[1,2,896,7168]{3,2,1,0:T(8,128)(2,1)} %param.13, pred[]{:T(512)S(6)} %eq.30), kind=kOutput, calls=%fused_computation.39 | convolution fusion | flops 514375680 | bytes 16357377 | tf_op jit(solution)/shard_map/dot_general | solution.py:71
  513.5 59.9 %all-reduce.13 = bf16[40,7168]{1,0:T(8,128)(2,1)} all-reduce(f32[40,7168]{1,0:T(8,128)} %fusion.49), channel_id=1, replica_groups=mesh['segment'=4,'vocab'=8] {'vocab'}, use_global_device_ids=true, to_apply=%region_20.21 | all-reduce | flops 286720 | bytes 1720320 | tf_op jit(solution)/shard_map/psum | solution.py:82
  574.6 8.1 %fusion.172 = (f32[40]{0:T(128)S(1)}, f32[40,1024]{1,0:T(8,128)S(1)}) fusion(bf16[7168,1024]{1,0:T(8,128)(2,1)} %all-gather.5.cloned.1.call-done, f32[7168]{0:T(1024)S(1)} %bitcast.105, f32[40]{0:T(128)S(1)} %add_rsqrt_fusion.7, bf16[40,7168]{1,0:T(8,128)(2,1)S(1)} %all-reduce.7), kind=kOutput, calls=%fused_computation.245 | convolution fusion | flops 588390336 | bytes 15446336 | tf_op jit(solution)/shard_map/dot_general | solution.py:93
  603.5 11.1 %all-gather.2 = f32[8,1,160]{2,1,0:T(1,128)S(1)} all-gather(f32[1,1,160]{2,1,0:T(1,128)S(1)} %select_n.451), channel_id=1, replica_groups=mesh['segment'=4,'vocab'=8] {'vocab'}, dimensions={0}, use_global_device_ids=true | all-gather | bytes 5760 | tf_op jit(solution)/shard_map/all_gather | solution.py:19
  615.5 9.6 %all-gather.1 = f32[8,1,160]{2,1,0:T(1,128)S(1)} all-gather(f32[1,1,160]{2,1,0:T(1,128)S(1)} %select_n.450), channel_id=1, replica_groups=mesh['segment'=4,'vocab'=8] {'vocab'}, dimensions={0}, use_global_device_ids=true | all-gather | bytes 5760 | tf_op jit(solution)/shard_map/all_gather | solution.py:19
  626.3 9.3 %all-gather = f32[8,1,160]{2,1,0:T(1,128)S(1)} all-gather(f32[1,1,160]{2,1,0:T(1,128)S(1)} %select_n.449), channel_id=1, replica_groups=mesh['segment'=4,'vocab'=8] {'vocab'}, dimensions={0}, use_global_device_ids=true | all-gather | bytes 5760 | tf_op jit(solution)/shard_map/all_gather | solution.py:19
  (200 shorter events, 76.1 us)
Async XLA Ops:
  6.5 568.1 %all-gather.5.cloned.1.call-start = ((), (), s32[]{:S(2)}) async-start(), calls=%async_computation | async-start | bytes 18350080 | tf_op jit(solution)/shard_map/all_gather | solution.py:57
  7.3 14.3 %copy-start.20 = (bf16[3,896]{1,0:T(4,128)(2,1)S(1)}, bf16[3,896]{1,0:T(4,128)(2,1)}, u32[]{:S(2)}) copy-start(bf16[3,896]{1,0:T(4,128)(2,1)} %param.15) | copy-start | bytes 16132
  7.7 100.1 %copy-start.15 = (f32[164,896]{1,0:T(8,128)}, f32[164,896]{1,0:T(8,128)S(1)}, u32[]{:S(2)}) copy-start(f32[164,896]{1,0:T(8,128)S(1)} %convert_element_type.133) | copy-start | bytes 1763332
  94.0 47.1 %collective-permute-start = (bf16[40,896]{1,0:T(8,128)(2,1)S(1)}, bf16[40,896]{1,0:T(8,128)(2,1)S(1)}, u32[]{:S(2)}, u32[]{:S(2)}) collective-permute-start(bf16[40,896]{1,0:T(8,128)(2,1)S(1)} %multiply_convert_fusion.23), channel_id=1, source_target_pairs={{0,8},{8,16},{16,24},{1,9},{9,17},{17,25},{2,10},{10,18},{18,26},{... | collective-permute-start | bytes 215048 | tf_op jit(solution)/shard_map/ppermute | solution.py:15
  99.6 32.9 %slice-start = ((s8[25690112]{0:T(1024)(128)(4,1)}), s8[4194304]{0:T(1024)(128)(4,1)S(1)}, s32[]{:S(2)}) async-start(s8[25690112]{0:T(1024)(128)(4,1)} %bitcast.103), calls=%async_computation.1 | async-start | bytes 8388608
  99.6 32.9 %slice-start.1 = ((s8[25690112]{0:T(1024)(128)(4,1)}), s8[4194304]{0:T(1024)(128)(4,1)S(1)}, s32[]{:S(2)}) async-start(s8[25690112]{0:T(1024)(128)(4,1)} %bitcast.103), calls=%async_computation.2 | async-start | bytes 8388608
  107.8 24.7 %slice-start.2 = ((s8[25690112]{0:T(1024)(128)(4,1)}), s8[4194304]{0:T(1024)(128)(4,1)S(1)}, s32[]{:S(2)}) async-start(s8[25690112]{0:T(1024)(128)(4,1)} %bitcast.103), calls=%async_computation.3 | async-start | bytes 8388608
  107.8 24.7 %slice-start.3 = ((s8[25690112]{0:T(1024)(128)(4,1)}), s8[4194304]{0:T(1024)(128)(4,1)S(1)}, s32[]{:S(2)}) async-start(s8[25690112]{0:T(1024)(128)(4,1)} %bitcast.103), calls=%async_computation.4 | async-start | bytes 8388608
  116.0 8.3 %copy-start.16 = (f32[164,896]{1,0:T(8,128)S(1)}, f32[164,896]{1,0:T(8,128)}, u32[]{:S(2)}) copy-start(f32[164,896]{1,0:T(8,128)} %copy-done.15) | copy-start | bytes 1763332
  116.0 16.5 %slice-start.4 = ((s8[25690112]{0:T(1024)(128)(4,1)}), s8[4194304]{0:T(1024)(128)(4,1)S(1)}, s32[]{:S(2)}) async-start(s8[25690112]{0:T(1024)(128)(4,1)} %bitcast.103), calls=%async_computation.5 | async-start | bytes 8388608
  116.0 16.5 %slice-start.5 = ((s8[25690112]{0:T(1024)(128)(4,1)}), s8[4194304]{0:T(1024)(128)(4,1)S(1)}, s32[]{:S(2)}) async-start(s8[25690112]{0:T(1024)(128)(4,1)} %bitcast.103), calls=%async_computation.6 | async-start | bytes 8388608
  124.3 8.2 %slice-start.6 = ((s8[25690112]{0:T(1024)(128)(4,1)}), s8[524288]{0:T(1024)(128)(4,1)S(1)}, s32[]{:S(2)}) async-start(s8[25690112]{0:T(1024)(128)(4,1)} %bitcast.103), calls=%async_computation.7 | async-start | bytes 1048576
  203.5 6.6 %copy-start.14 = (f32[40,7168]{1,0:T(8,128)S(1)}, f32[40,7168]{1,0:T(8,128)}, u32[]{:S(2)}) copy-start(f32[40,7168]{1,0:T(8,128)} %fusion.8) | copy-start | bytes 3440644
  203.5 6.5 %copy-start.6 = (f32[40,7168]{1,0:T(8,128)S(1)}, f32[40,7168]{1,0:T(8,128)}, u32[]{:S(2)}) copy-start(f32[40,7168]{1,0:T(8,128)} %copy-done.5) | copy-start | bytes 3440644
  203.9 6.1 collective-permute-start.1
  278.1 6.0 collective-permute-start.2
  350.4 6.6 %copy-start.12 = (f32[40,7168]{1,0:T(8,128)S(1)}, f32[40,7168]{1,0:T(8,128)}, u32[]{:S(2)}) copy-start(f32[40,7168]{1,0:T(8,128)} %fusion.4) | copy-start | bytes 3440644
  350.5 6.5 %copy-start.8 = (f32[40,7168]{1,0:T(8,128)S(1)}, f32[40,7168]{1,0:T(8,128)}, u32[]{:S(2)}) copy-start(f32[40,7168]{1,0:T(8,128)} %copy-done.7) | copy-start | bytes 3440644
  350.8 6.1 collective-permute-start.3
  424.3 6.4 copy-start.11
  424.8 6.0 collective-permute-start.4
  497.6 7.6 %copy-start.10 = (f32[40,7168]{1,0:T(8,128)S(1)}, f32[40,7168]{1,0:T(8,128)}, u32[]{:S(2)}) copy-start(f32[40,7168]{1,0:T(8,128)} %copy-done.9) | copy-start | bytes 3440644
  499.2 6.0 collective-permute-start.5
  574.6 9.3 %copy-start = (bf16[7168,1024]{1,0:T(8,128)(2,1)S(1)}, bf16[7168,1024]{1,0:T(8,128)(2,1)}, u32[]{:S(2)}) copy-start(bf16[7168,1024]{1,0:T(8,128)(2,1)} %all-gather.5.cloned.1.call-done) | copy-start | bytes 44040196
  (13 other events, 33.8 us)
Sparse Core Ops, SparseCore 0:
  9.2 141.4 all-gather.4
where the time goes:
time: 648 us; the launch traced here: 644 us
  blocking collectives  454 us (70%)
  matrix products  123 us (19%)
  waiting for transfers between devices  18.1 us (3%)
  between operations  14.3 us (2%)
  starting transfers between devices  13.8 us (2%)
  other arithmetic  11.7 us (2%)
  local copies, waits for them, and re-layouts  7.92 us (1%)
    psum x7, blocking collectives, per_device(): lax.psum(jnp.where(leading, placed, partial_value), 'vocab')  411 us
    dot_general x7, matrix products, per_device(): jnp.dot(incoming, module_block[0], preferred_element_type=jnp.float32)  50.8 us
    dot_general x7, matrix products, per_device(): jnp.dot(embed_normed, module_block[1], preferred_element_type=jnp.float32)  47.2 us
    all_gather x3, blocking collectives, combined_all(): everything = jax.tree.map(lambda part: lax.all_gather(part, axis), shard)  30.1 us
    dot_general x7, matrix products, per_device(): logits = jnp.dot(head_input, whole_head, preferred_element_type=jnp.float32)  25.3 us
    ppermute x6, waiting for transfers between devices, passed_along(): return lax.ppermute(block, axis, route)  17.4 us
    psum x1, blocking collectives, per_device(): lax.psum(jnp.sum(embed_float * embed_float, axis=1), 'vocab')  13.8 us
    ppermute x6, starting transfers between devices, passed_along(): return lax.ppermute(block, axis, route)  13.8 us
  transfers between devices with their start and end apart: 7, of which 5 were waited for; matrix products, arithmetic and copies ran while one was open for 17% of the time, Pallas kernels for 0%

commit v1 on v0

--- a/solution.py
+++ b/solution.py
@@ -7,6 +7,11 @@
 TOK = 160
 MICRO = 4
 EPSILON = 1e-06
+
+
+def add_all(x, name):
+    parts = lax.all_gather(x, name)
+    return jnp.sum(parts, axis=0)
 
 
 def passed_along(block, axis, distance):
@@ -79,9 +84,7 @@
             shard_index * local_width,
             1,
         )
-        full_rows = lax.psum(jnp.where(leading, placed, partial_value), "vocab").astype(
-            jnp.bfloat16
-        )
+        full_rows = add_all(jnp.where(leading, placed, partial_value), "vocab").astype(jnp.bfloat16)
         rows_float = full_rows.astype(jnp.float32)
         inverse_rms = lax.rsqrt(jnp.mean(rows_float * rows_float, axis=1, keepdims=True) + EPSILON)
         head_input = (rows_float * inverse_rms * out_scaling).astype(jnp.bfloat16)

time: 648 us -> 948 us (1.46)
  waiting for transfers between devices: 18.1 us -> 678 us
  blocking collectives: 454 us -> 41.9 us
  other arithmetic: 11.7 us -> 46.1 us
  matrix products: 123 us -> 134 us
    all_gather x0 -> x7, waiting for transfers between devices: none -> 546 us  [add_all(): parts = lax.all_gather(x, name)]
    psum x7 -> x0, blocking collectives: 411 us -> none  [per_device(): lax.psum(jnp.where(leading, placed, partial_value), 'vocab')]
    all_gather x1, waiting for transfers between devices: 0.02 us -> 118 us  [per_device(): whole_head = lax.all_gather(head_weight, 'segment', axis=0, tiled=True)]
    reduce_sum x0 -> x7, other arithmetic: none -> 29.4 us  [add_all(): return jnp.sum(parts, axis=0)]
  transfers between devices with their start and end apart: 7 -> 14, of which waited for: 5 -> 14; matrix products, arithmetic and copies ran while one was open for 17% -> 9% of each run, Pallas kernels for 0% -> 0%
where the time goes in v1:
time: 948 us; the launch traced here: 939 us
  waiting for transfers between devices  678 us (72%)
  matrix products  134 us (14%)
  other arithmetic  46.1 us (5%)
  blocking collectives  41.9 us (4%)
  starting transfers between devices  19.7 us (2%)
  between operations  14.5 us (2%)
    all_gather x7, waiting for transfers between devices, add_all(): parts = lax.all_gather(x, name)  546 us
    all_gather x1, waiting for transfers between devices, per_device(): whole_head = lax.all_gather(head_weight, 'segment', axis=0, tiled=True)  118 us
    dot_general x7, matrix products, per_device(): jnp.dot(incoming, module_block[0], preferred_element_type=jnp.float32)  57.7 us
    dot_general x7, matrix products, per_device(): jnp.dot(embed_normed, module_block[1], preferred_element_type=jnp.float32)  46.3 us
    dot_general x7, matrix products, per_device(): logits = jnp.dot(head_input, whole_head, preferred_element_type=jnp.float32)  30.4 us
    reduce_sum x7, other arithmetic, add_all(): return jnp.sum(parts, axis=0)  29.4 us
    all_gather x3, blocking collectives, combined_all(): everything = jax.tree.map(lambda part: lax.all_gather(part, axis), shard)  28.1 us
  transfers between devices with their start and end apart: 14, of which 14 were waited for; matrix products, arithmetic and copies ran while one was open for 9% of the time, Pallas kernels for 0%

profile of v1, /device:TPU:5, one launch (start us, length us, event | category | flops | bytes accessed | tf_op | source)
XLA Modules:
  0.0 938.7 jit_solution(6683939558734742536)
XLA Ops:
  8.9 13.8 %psum.7 = f32[164]{0:T(256)S(1)} all-reduce(f32[164]{0:T(256)S(1)} %multiply_reduce_fusion.6), channel_id=1, replica_groups=mesh['segment'=4,'vocab'=8] {'vocab'}, use_global_device_ids=true, to_apply=%region_1.0 | all-reduce | flops 164 | bytes 1312 | tf_op jit(solution)/shard_map/psum | solution.py:50
  29.8 8.0 fusion.67
  44.5 83.4 %all-gather.21.cloned.1.call-done = f32[320,7168]{1,0:T(8,128)} async-done(((f32[40,7168]{1,0:T(8,128)}), f32[320,7168]{1,0:T(8,128)}) %all-gather.21.cloned.1.call-update) | async-done | bytes 9175056 | tf_op jit(solution)/shard_map/all_gather | solution.py:13
  138.9 8.0 fusion.64
  152.9 81.1 %all-gather.23.cloned.1.call-done = f32[320,7168]{1,0:T(8,128)} async-done(((f32[40,7168]{1,0:T(8,128)}), f32[320,7168]{1,0:T(8,128)}) %all-gather.23.cloned.1.call-update) | async-done | bytes 9175056 | tf_op jit(solution)/shard_map/all_gather | solution.py:13
  244.9 8.0 fusion.61
  259.5 80.5 %all-gather.25.cloned.1.call-done = f32[320,7168]{1,0:T(8,128)} async-done(((f32[40,7168]{1,0:T(8,128)}), f32[320,7168]{1,0:T(8,128)}) %all-gather.25.cloned.1.call-update) | async-done | bytes 9175056 | tf_op jit(solution)/shard_map/all_gather | solution.py:13
  351.0 8.0 fusion.58
  359.1 6.0 fusion.4
  365.1 81.0 %all-gather.27.cloned.1.call-done = f32[320,7168]{1,0:T(8,128)} async-done(((f32[40,7168]{1,0:T(8,128)}), f32[320,7168]{1,0:T(8,128)}) %all-gather.27.cloned.1.call-update) | async-done | bytes 9175056 | tf_op jit(solution)/shard_map/all_gather | solution.py:13
  457.0 8.0 fusion.55
  465.1 8.2 fusion.2
  473.3 78.9 %all-gather.29.cloned.1.call-done = f32[320,7168]{1,0:T(8,128)} async-done(((f32[40,7168]{1,0:T(8,128)}), f32[320,7168]{1,0:T(8,128)}) %all-gather.29.cloned.1.call-update) | async-done | bytes 9175056 | tf_op jit(solution)/shard_map/all_gather | solution.py:13
  563.2 8.0 fusion.52
  572.0 8.3 fusion
  580.4 77.9 %all-gather.31.cloned.1.call-done = f32[320,7168]{1,0:T(8,128)} async-done(((f32[40,7168]{1,0:T(8,128)}), f32[320,7168]{1,0:T(8,128)}) %all-gather.31.cloned.1.call-update) | async-done | bytes 9175056 | tf_op jit(solution)/shard_map/all_gather | solution.py:13
  669.3 9.6 %fusion.49 = f32[40,7168]{1,0:T(8,128)} fusion(f32[40,7168]{1,0:T(8,128)S(1)} %convert_dynamic-update-slice_fusion, f32[40,7168]{1,0:T(8,128)S(1)} %copy-done.1, bf16[40,896]{1,0:T(8,128)(2,1)S(1)} %collective-permute-done.5, bf16[1,2,896,7168]{3,2,1,0:T(8,128)(2,1)} %param.13, pred[]{:T(512)S(6)} %eq.30), kind=kOutput, calls=%fused_computation.39 | convolution fusion | flops 514375680 | bytes 16357377 | tf_op jit(solution)/shard_map/dot_general | solution.py:76
  679.9 118.0 %all-gather.19.cloned.1.call-done = bf16[7168,1024]{1,0:T(8,128)(2,1)} async-done(((bf16[1792,1024]{1,0:T(8,128)(2,1)}), bf16[7168,1024]{1,0:T(8,128)(2,1)}) %all-gather.19.cloned.1.call-update) | async-done | bytes 14680080 | tf_op jit(solution)/shard_map/all_gather | solution.py:62
  797.9 8.1 fusion.172
  825.2 63.5 %all-gather.33.cloned.1.call-done = f32[320,7168]{1,0:T(8,128)} async-done(((f32[40,7168]{1,0:T(8,128)}), f32[320,7168]{1,0:T(8,128)}) %all-gather.33.cloned.1.call-update) | async-done | bytes 9175056 | tf_op jit(solution)/shard_map/all_gather | solution.py:13
  893.1 8.0 fusion.178
  901.4 9.2 all-gather.7
  911.1 9.7 %all-gather.8 = f32[8,1,160]{2,1,0:T(1,128)S(1)} all-gather(f32[1,1,160]{2,1,0:T(1,128)S(1)} %select_n.450), channel_id=1, replica_groups=mesh['segment'=4,'vocab'=8] {'vocab'}, dimensions={0}, use_global_device_ids=true | all-gather | bytes 5760 | tf_op jit(solution)/shard_map/all_gather | solution.py:24
  921.1 9.1 all-gather.9
  (176 shorter events, 122.0 us)
Async XLA Ops:
  6.5 16.2 %copy-start.5 = (bf16[3,896]{1,0:T(4,128)(2,1)S(1)}, bf16[3,896]{1,0:T(4,128)(2,1)}, u32[]{:S(2)}) copy-start(bf16[3,896]{1,0:T(4,128)(2,1)} %param.15) | copy-start | bytes 16132
  6.5 121.4 %all-gather.21.cloned.1.call-start = ((), (), s32[]{:S(2)}) async-start(), calls=%async_computation.1 | async-start | bytes 10321920 | tf_op jit(solution)/shard_map/all_gather | solution.py:13
  7.6 246.0 %copy-start.3 = (f32[164,896]{1,0:T(8,128)}, f32[164,896]{1,0:T(8,128)S(1)}, u32[]{:S(2)}) copy-start(f32[164,896]{1,0:T(8,128)S(1)} %convert_element_type.133) | copy-start | bytes 1763332
  37.8 0.7 copy-start.6
  37.8 196.2 %all-gather.23.cloned.1.call-start = ((), (), s32[]{:S(2)}) async-start(), calls=%async_computation.2 | async-start | bytes 10321920 | tf_op jit(solution)/shard_map/all_gather | solution.py:13
  132.5 6.3 collective-permute-start
  146.9 193.2 %all-gather.25.cloned.1.call-start = ((), (), s32[]{:S(2)}) async-start(), calls=%async_computation.3 | async-start | bytes 10321920 | tf_op jit(solution)/shard_map/all_gather | solution.py:13
  238.6 6.3 collective-permute-start.1
  253.0 193.1 %all-gather.27.cloned.1.call-start = ((), (), s32[]{:S(2)}) async-start(), calls=%async_computation.4 | async-start | bytes 10321920 | tf_op jit(solution)/shard_map/all_gather | solution.py:13
  344.7 6.3 collective-permute-start.2
  359.0 193.1 %all-gather.29.cloned.1.call-start = ((), (), s32[]{:S(2)}) async-start(), calls=%async_computation.5 | async-start | bytes 10321920 | tf_op jit(solution)/shard_map/all_gather | solution.py:13
  450.7 6.3 collective-permute-start.3
  465.1 193.3 %all-gather.31.cloned.1.call-start = ((), (), s32[]{:S(2)}) async-start(), calls=%async_computation.6 | async-start | bytes 10321920 | tf_op jit(solution)/shard_map/all_gather | solution.py:13
  556.7 6.6 copy-start.2
  556.8 6.4 collective-permute-start.4
  571.2 226.6 %all-gather.19.cloned.1.call-start = ((), (), s32[]{:S(2)}) async-start(), calls=%async_computation | async-start | bytes 18350080 | tf_op jit(solution)/shard_map/all_gather | solution.py:62
  572.0 316.7 %all-gather.33.cloned.1.call-start = ((), (), s32[]{:S(2)}) async-start(), calls=%async_computation.7 | async-start | bytes 10321920 | tf_op jit(solution)/shard_map/all_gather | solution.py:13
  662.6 6.7 copy-start.1
  663.0 6.3 collective-permute-start.5
  678.9 0.7 copy-start.4
  678.9 0.8 copy-start.7
  797.9 9.5 %copy-start = (bf16[7168,1024]{1,0:T(8,128)(2,1)S(1)}, bf16[7168,1024]{1,0:T(8,128)(2,1)}, u32[]{:S(2)}) copy-start(bf16[7168,1024]{1,0:T(8,128)(2,1)} %all-gather.19.cloned.1.call-done) | copy-start | bytes 44040196
Sparse Core Ops, SparseCore 0:
  38.0 89.9 all-gather.20
  147.0 86.9 all-gather.22
  253.1 86.9 all-gather.24
  359.1 86.9 all-gather.26
  465.2 86.9 all-gather.28
  571.4 86.9 all-gather.30
  660.2 137.6 all-gather.18
  799.5 89.1 all-gather.32
